TPU v7x, 32 devices: a whole 2x2x4 slice. The times are simulated.
32 devices in a mesh: seq: 16 (over z, y, core), head: 2 (over x).
Axes of the slice: x: 2, y: 2, z: 4, core: 2. Of those that a mesh axis runs over, the one named last changes fastest.
Arguments:
- qkv: bfloat16 [3, 2048, 1024], P(None, ('seq', 'head')), may hold values from -128 to 128
- token_rate: float32 [2048, 2], P('seq', 'head'), may hold values from 0.1 to 1
- head_rate: float32 [2], P('head'), may hold values from 0.5 to 2
- fast_state: float32 [3, 2, 512, 512], P(None, 'head', 'seq'), may hold values from -0.25 to 0.25
Outputs:
- combined: bfloat16 [2048, 1024], P(('seq', 'head'))
- new_state: float32 [3, 2, 512, 512], P(None, 'head', 'seq')
All inputs are finite; a program needn't handle non-finite values.
Results may differ from a plain program's by a relative error of at most 0.017.
Values may be sent and summed in bfloat16 or wider, within the bound.
A program may use at most 64 MiB of HBM per device.

v0:
```python
import jax
import jax.numpy as jnp
from jax import lax
from jax.sharding import PartitionSpec as P

WINDOW = 1024
NS_STEPS = 2
ns_first = 3.4445
ns_second = -4.775
ns_third = 2.0315
rms_eps = 1e-06
norm_eps = 1e-07
precise = lax.Precision.HIGHEST


def from_behind(block, axis, distance):
    devices = range(lax.axis_size(axis))
    route = [(i - distance, i) for i in devices if i - distance in devices]
    return lax.ppermute(block, axis, route)


def rms_scaled(values):
    return values * lax.rsqrt(jnp.mean(values * values, axis=-1, keepdims=True) + rms_eps)


def contract_last(left_side, right_side):
    return lax.dot_general(
        left_side, right_side, (((1,), (1,)), ((), ())), preferred_element_type=jnp.float32
    )


def contract_first(left_side, right_side):
    return lax.dot_general(
        left_side, right_side, (((0,), (0,)), ((), ())), preferred_element_type=jnp.float32
    )


def head_gradient(key_norm, signal, weight_piece):
    gate_act = contract_last(key_norm, weight_piece[0])
    up_act = contract_last(key_norm, weight_piece[1])
    active = (jax.nn.silu(gate_act) * up_act).astype(jnp.bfloat16)
    back_grad = contract_last(signal, weight_piece[2])
    sigmoid_gate = jax.nn.sigmoid(gate_act)
    grad_gate = (
        back_grad * up_act * sigmoid_gate * (1.0 + gate_act * (1.0 - sigmoid_gate))
    ).astype(jnp.bfloat16)
    grad_up = (back_grad * jax.nn.silu(gate_act)).astype(jnp.bfloat16)
    return jnp.stack(
        [
            contract_first(grad_gate, key_norm),
            contract_first(grad_up, key_norm),
            contract_first(active, signal),
        ]
    )


def gram_times(gram_matrix, section_number, row_block):
    if section_number == 0:
        return jnp.einsum("mij,mjk->mik", row_block, gram_matrix, precision=precise)
    once_moved = gram_times(gram_matrix, section_number - 1, row_block)
    return poly_times(
        gram_matrix, section_number - 1, poly_times(gram_matrix, section_number - 1, once_moved)
    )


def poly_times(gram_matrix, section_number, row_block):
    moved_once = gram_times(gram_matrix, section_number, row_block)
    moved_twice = gram_times(gram_matrix, section_number, moved_once)
    return ns_first * row_block + ns_second * moved_once + ns_third * moved_twice


def shards(qkv, token_rate, head_rate, fast_state):
    grouped = lax.all_to_all(qkv, "head", split_axis=2, concat_axis=1, tiled=True)
    tok_rows = grouped.shape[1]
    head_dim = grouped.shape[2]
    seq_index = lax.axis_index("seq")
    state_rows = fast_state.shape[2]
    query_norm = rms_scaled(grouped[0].astype(jnp.float32)).astype(jnp.bfloat16)
    key_norm = rms_scaled(grouped[1].astype(jnp.float32)).astype(jnp.bfloat16)
    signal = (-token_rate * grouped[2].astype(jnp.float32)).astype(jnp.bfloat16)
    old_state = fast_state[:, 0]
    old_low = old_state.astype(jnp.bfloat16)
    partial_value = head_gradient(
        key_norm, signal, lax.all_gather(old_low, "seq", axis=1, tiled=True)
    )
    summed = lax.psum(partial_value, "seq")
    frob_norm = jnp.sqrt(jnp.sum(summed * summed, axis=(1, 2), keepdims=True))
    normalized = summed / (frob_norm + norm_eps)
    gram_matrix = jnp.einsum("mij,mkj->mik", normalized, normalized, precision=precise)
    hidden_units = gram_matrix.shape[1]
    selector = (
        jnp.arange(hidden_units, dtype=jnp.int32)[None, :]
        == seq_index * state_rows + jnp.arange(state_rows, dtype=jnp.int32)[:, None]
    ).astype(jnp.float32)
    row_block = jnp.broadcast_to(selector, (3, state_rows, hidden_units))
    for section_number in range(NS_STEPS - 1, -1, -1):
        row_block = poly_times(gram_matrix, section_number, row_block)
    final_rows = jnp.einsum("mij,mjk->mik", row_block, normalized, precision=precise)
    new_rows = old_state - head_rate[0] * final_rows
    weight_piece = lax.all_gather(new_rows.astype(jnp.bfloat16), "seq", axis=1, tiled=True)
    gate_act = contract_last(query_norm, weight_piece[0])
    up_act = contract_last(query_norm, weight_piece[1])
    active = (jax.nn.silu(gate_act) * up_act).astype(jnp.bfloat16)
    fast_out = jnp.dot(active, weight_piece[2], preferred_element_type=jnp.float32)
    key_value = grouped[1:3]
    reach_blocks = WINDOW // tok_rows
    earlier = [from_behind(key_value, "seq", distance) for distance in range(reach_blocks, 0, -1)]
    context = jnp.concatenate(earlier + [key_value], axis=1)
    scores = contract_last(grouped[0], context[0]) * head_dim ** (-0.5)
    query_pos = seq_index * tok_rows + jnp.arange(tok_rows, dtype=jnp.int32)[:, None]
    key_pos = (
        seq_index * tok_rows - WINDOW + jnp.arange(WINDOW + tok_rows, dtype=jnp.int32)[None, :]
    )
    visible = (key_pos <= query_pos) & (key_pos > query_pos - WINDOW) & (key_pos >= 0)
    scores = jnp.where(visible, scores, -jnp.inf)
    row_max = jnp.max(scores, axis=1, keepdims=True)
    exp_scores = jnp.exp(scores - row_max)
    weights = (exp_scores / jnp.sum(exp_scores, axis=1, keepdims=True)).astype(jnp.bfloat16)
    attention = jnp.dot(weights, context[1], preferred_element_type=jnp.float32)
    combined = (attention + fast_out).astype(jnp.bfloat16)
    tokens_back = lax.all_to_all(combined, "head", split_axis=0, concat_axis=1, tiled=True)
    return (tokens_back, new_rows[:, None])


def solution(mesh):
    return jax.shard_map(
        shards,
        mesh=mesh,
        in_specs=(
            P(None, ("seq", "head"), None),
            P("seq", "head"),
            P("head"),
            P(None, "head", "seq", None),
        ),
        out_specs=(P(("seq", "head"), None), P(None, "head", "seq", None)),
        check_vma=False,
    )
```

profile of v0, /device:TPU:16, one launch (start us, length us, event | category | flops | bytes accessed | tf_op | source)
XLA Modules:
  0.0 289.8 jit_solution(17737878514424476235)
XLA Ops:
  11.9 3.5 %all-to-all-start = ((bf16[2,2,49152]{2,1,0:T(2,128)(2,1)}), bf16[2,2,49152]{2,1,0:T(2,128)(2,1)S(1)}, u32[]{:S(2)}, u32[]{:S(2)}) async-start(bf16[2,2,49152]{2,1,0:T(2,128)(2,1)} %reshape.124), calls=%async_computation | async-start | bytes 786432 | tf_op jit(solution)/shard_map/all_to_all | solution.py:73
  15.5 6.7 %all-to-all-done = bf16[2,2,49152]{2,1,0:T(2,128)(2,1)S(1)} async-done(((bf16[2,2,49152]{2,1,0:T(2,128)(2,1)}), bf16[2,2,49152]{2,1,0:T(2,128)(2,1)S(1)}, u32[]{:S(2)}, u32[]{:S(2)}) %all-to-all-start) | async-done | bytes 393248 | tf_op jit(solution)/shard_map/all_to_all | solution.py:73
  24.0 25.6 %all-gather.3.cloned.1.call-done = bf16[3,512,512]{2,1,0:T(8,128)(2,1)} async-done(((bf16[3,32,512]{2,1,0:T(8,128)(2,1)}), bf16[3,512,512]{2,1,0:T(8,128)(2,1)}) %all-gather.3.cloned.1.call-update) | async-done | bytes 1572880 | tf_op jit(solution)/shard_map/all_gather | solution.py:84
  54.7 2.0 pad_maximum_fusion
  57.8 102.6 %all-reduce.2.cloned.1.call-done = f32[3,512,512]{2,1,0:T(8,128)} async-done(((f32[3,512,512]{2,1,0:T(8,128)}), f32[3,512,512]{2,1,0:T(8,128)}) %all-reduce.2.cloned.1.call-update) | async-done | bytes 3145744 | tf_op jit(solution)/shard_map/psum | solution.py:86
  160.3 2.5 multiply_reduce_fusion
  163.2 5.6 %fusion.15 = f32[3,512,512]{2,1,0:T(8,128)S(1)} fusion(f32[3,512,512]{2,1,0:T(8,128)S(1)} %copy-done, f32[3]{0:T(128)S(1)} %sqrt_add_fusion), kind=kOutput, calls=%fused_computation.33 | convolution fusion | flops 4832624640 | bytes 6291468 | tf_op jit(solution)/shard_map/mij,mkj->mik/dot_general | solution.py:89
  168.8 1.9 fusion.35
  170.7 1.9 fusion.48
  172.6 1.9 fusion.12
  174.5 1.9 fusion.49
  176.4 2.1 fusion.11
  180.4 1.9 fusion.51
  182.3 1.9 fusion.10
  186.2 1.9 fusion.9
  188.1 1.9 fusion.53
  190.0 2.1 fusion.6
  192.1 2.8 fusion.46
  196.3 1.9 collective-permute-start.1
  198.2 2.9 collective-permute-start.2
  201.1 1.9 collective-permute-start.3
  203.1 1.9 collective-permute-start.4
  205.0 2.3 collective-permute-done
  207.3 1.9 collective-permute-start.5
  209.2 12.2 %collective-permute-start.6 = (bf16[2,128,512]{2,1,0:T(8,128)(2,1)S(1)}, bf16[2,128,512]{2,1,0:T(8,128)(2,1)S(1)}, u32[]{:S(2)}, u32[]{:S(2)}) collective-permute-start(bf16[2,128,512]{2,1,0:T(8,128)(2,1)S(1)} %bitcast.119), channel_id=1, source_target_pairs={{0,4},{2,6},{4,8},{6,10},{8,12},{10,14},{12,16},{14,18},{16,20},{1... | collective-permute-start | bytes 786440 | tf_op jit(solution)/shard_map/ppermute | solution.py:19
  221.8 13.3 %collective-permute-start.7 = (bf16[2,128,512]{2,1,0:T(8,128)(2,1)S(1)}, bf16[2,128,512]{2,1,0:T(8,128)(2,1)S(1)}, u32[]{:S(2)}, u32[]{:S(2)}) collective-permute-start(bf16[2,128,512]{2,1,0:T(8,128)(2,1)S(1)} %bitcast.120), channel_id=1, source_target_pairs={{0,2},{2,4},{4,6},{6,8},{8,10},{10,12},{12,14},{14,16},{16,18},{18... | collective-permute-start | bytes 786440 | tf_op jit(solution)/shard_map/ppermute | solution.py:19
  235.2 8.6 %collective-permute-done.4 = bf16[2,128,512]{2,1,0:T(8,128)(2,1)S(1)} collective-permute-done((bf16[2,128,512]{2,1,0:T(8,128)(2,1)S(1)}, bf16[2,128,512]{2,1,0:T(8,128)(2,1)S(1)}, u32[]{:S(2)}, u32[]{:S(2)}) %collective-permute-start.4) | collective-permute-done | bytes 262176 | tf_op jit(solution)/shard_map/ppermute | solution.py:19
  243.9 2.9 collective-permute-done.5
  246.8 20.7 %collective-permute-done.6 = bf16[2,128,512]{2,1,0:T(8,128)(2,1)S(1)} collective-permute-done((bf16[2,128,512]{2,1,0:T(8,128)(2,1)S(1)}, bf16[2,128,512]{2,1,0:T(8,128)(2,1)S(1)}, u32[]{:S(2)}, u32[]{:S(2)}) %collective-permute-start.6) | collective-permute-done | bytes 262176 | tf_op jit(solution)/shard_map/ppermute | solution.py:19
  267.5 2.3 collective-permute-done.7
  271.9 2.4 fusion.14
  275.6 7.0 %all_to_all.34 = bf16[2,64,512]{2,1,0:T(8,128)(2,1)S(1)} all-to-all(bf16[2,64,512]{2,1,0:T(8,128)(2,1)S(1)} %bitcast.127), channel_id=1, replica_groups=mesh['seq'=16,'head'=2] {'head'}, dimensions={0} | all-to-all | bytes 262144 | tf_op jit(solution)/shard_map/all_to_all | solution.py:121
  (61 shorter events, 22.1 us)
Async XLA Ops:
  7.2 8.2 %copy-start.2 = (f32[128,1]{0,1:T(1,128)S(1)}, f32[128,1]{0,1:T(1,128)}, u32[]{:S(2)}) copy-start(f32[128,1]{0,1:T(1,128)} %param.5) | copy-start | bytes 1540
  7.2 42.5 %all-gather.3.cloned.1.call-start = ((), (), s32[]{:S(2)}) async-start(), calls=%async_computation.2 | async-start | bytes 1671168 | tf_op jit(solution)/shard_map/all_gather | solution.py:84
  11.9 10.3 %all-to-all-start = ((bf16[2,2,49152]{2,1,0:T(2,128)(2,1)}), bf16[2,2,49152]{2,1,0:T(2,128)(2,1)S(1)}, u32[]{:S(2)}, u32[]{:S(2)}) async-start(bf16[2,2,49152]{2,1,0:T(2,128)(2,1)} %reshape.124), calls=%async_computation | async-start | bytes 786432 | tf_op jit(solution)/shard_map/all_to_all | solution.py:73
  15.3 145.0 %all-reduce.2.cloned.1.call-start = ((), (), s32[]{:S(2)}) async-start(), calls=%async_computation.3 | async-start | bytes 6291456 | tf_op jit(solution)/shard_map/psum | solution.py:86
  56.7 213.8 %all-gather.5.cloned.1.call-start = ((), (), s32[]{:S(2)}) async-start(), calls=%async_computation.4 | async-start | bytes 1671168 | tf_op jit(solution)/shard_map/all_gather | solution.py:100
  160.3 2.8 copy-start
  188.1 4.1 %copy-start.1 = (f32[3,1,32,512]{3,2,1,0:T(8,128)S(1)}, f32[3,1,32,512]{3,2,1,0:T(8,128)}, u32[]{:S(2)}) copy-start(f32[3,1,32,512]{3,2,1,0:T(8,128)} %param.7) | copy-start | bytes 589828
  195.0 12.3 %collective-permute-start = (bf16[2,128,512]{2,1,0:T(8,128)(2,1)S(1)}, bf16[2,128,512]{2,1,0:T(8,128)(2,1)S(1)}, u32[]{:S(2)}, u32[]{:S(2)}) collective-permute-start(bf16[2,128,512]{2,1,0:T(8,128)(2,1)S(1)} %bitcast.113), channel_id=1, source_target_pairs={{0,16},{2,18},{4,20},{6,22},{8,24},{10,26},{12,28},{14,30},{1,17},... | collective-permute-start | bytes 786440 | tf_op jit(solution)/shard_map/ppermute | solution.py:19
  196.3 12.9 %collective-permute-start.1 = (bf16[2,128,512]{2,1,0:T(8,128)(2,1)S(1)}, bf16[2,128,512]{2,1,0:T(8,128)(2,1)S(1)}, u32[]{:S(2)}, u32[]{:S(2)}) collective-permute-start(bf16[2,128,512]{2,1,0:T(8,128)(2,1)S(1)} %bitcast.114), channel_id=1, source_target_pairs={{0,14},{2,16},{4,18},{6,20},{8,22},{10,24},{12,26},{14,28},{16,30}... | collective-permute-start | bytes 786440 | tf_op jit(solution)/shard_map/ppermute | solution.py:19
  198.2 23.6 %collective-permute-start.2 = (bf16[2,128,512]{2,1,0:T(8,128)(2,1)S(1)}, bf16[2,128,512]{2,1,0:T(8,128)(2,1)S(1)}, u32[]{:S(2)}, u32[]{:S(2)}) collective-permute-start(bf16[2,128,512]{2,1,0:T(8,128)(2,1)S(1)} %bitcast.115), channel_id=1, source_target_pairs={{0,12},{2,14},{4,16},{6,18},{8,20},{10,22},{12,24},{14,26},{16,28}... | collective-permute-start | bytes 786440 | tf_op jit(solution)/shard_map/ppermute | solution.py:19
  201.1 34.1 %collective-permute-start.3 = (bf16[2,128,512]{2,1,0:T(8,128)(2,1)S(1)}, bf16[2,128,512]{2,1,0:T(8,128)(2,1)S(1)}, u32[]{:S(2)}, u32[]{:S(2)}) collective-permute-start(bf16[2,128,512]{2,1,0:T(8,128)(2,1)S(1)} %bitcast.116), channel_id=1, source_target_pairs={{0,10},{2,12},{4,14},{6,16},{8,18},{10,20},{12,22},{14,24},{16,26}... | collective-permute-start | bytes 786440 | tf_op jit(solution)/shard_map/ppermute | solution.py:19
  203.1 40.8 %collective-permute-start.4 = (bf16[2,128,512]{2,1,0:T(8,128)(2,1)S(1)}, bf16[2,128,512]{2,1,0:T(8,128)(2,1)S(1)}, u32[]{:S(2)}, u32[]{:S(2)}) collective-permute-start(bf16[2,128,512]{2,1,0:T(8,128)(2,1)S(1)} %bitcast.117), channel_id=1, source_target_pairs={{0,8},{2,10},{4,12},{6,14},{8,16},{10,18},{12,20},{14,22},{16,24},... | collective-permute-start | bytes 786440 | tf_op jit(solution)/shard_map/ppermute | solution.py:19
  207.3 39.5 %collective-permute-start.5 = (bf16[2,128,512]{2,1,0:T(8,128)(2,1)S(1)}, bf16[2,128,512]{2,1,0:T(8,128)(2,1)S(1)}, u32[]{:S(2)}, u32[]{:S(2)}) collective-permute-start(bf16[2,128,512]{2,1,0:T(8,128)(2,1)S(1)} %bitcast.118), channel_id=1, source_target_pairs={{0,6},{2,8},{4,10},{6,12},{8,14},{10,16},{12,18},{14,20},{16,22},{... | collective-permute-start | bytes 786440 | tf_op jit(solution)/shard_map/ppermute | solution.py:19
  209.2 58.3 %collective-permute-start.6 = (bf16[2,128,512]{2,1,0:T(8,128)(2,1)S(1)}, bf16[2,128,512]{2,1,0:T(8,128)(2,1)S(1)}, u32[]{:S(2)}, u32[]{:S(2)}) collective-permute-start(bf16[2,128,512]{2,1,0:T(8,128)(2,1)S(1)} %bitcast.119), channel_id=1, source_target_pairs={{0,4},{2,6},{4,8},{6,10},{8,12},{10,14},{12,16},{14,18},{16,20},{1... | collective-permute-start | bytes 786440 | tf_op jit(solution)/shard_map/ppermute | solution.py:19
  221.8 48.0 %collective-permute-start.7 = (bf16[2,128,512]{2,1,0:T(8,128)(2,1)S(1)}, bf16[2,128,512]{2,1,0:T(8,128)(2,1)S(1)}, u32[]{:S(2)}, u32[]{:S(2)}) collective-permute-start(bf16[2,128,512]{2,1,0:T(8,128)(2,1)S(1)} %bitcast.120), channel_id=1, source_target_pairs={{0,2},{2,4},{4,6},{6,8},{8,10},{10,12},{12,14},{14,16},{16,18},{18... | collective-permute-start | bytes 786440 | tf_op jit(solution)/shard_map/ppermute | solution.py:19
Sparse Core Ops, SparseCore 0:
  10.7 38.8 all-gather.2
  56.8 103.4 all-reduce.1
  195.1 53.1 all-gather.4
where the time goes:
time: 290 us
  waiting for transfers between devices  172 us (59%)
  matrix products  42.2 us (15%)
  starting transfers between devices  41.2 us (14%)
  between operations  14.8 us (5%)
  blocking collectives  7 us (2%)
  other arithmetic  6.92 us (2%)
  local copies, waits for them, and re-layouts  5.59 us (2%)
    psum x1, waiting for transfers between devices, shards(): summed = lax.psum(partial_value, 'seq')  103 us
    ppermute x8, starting transfers between devices, from_behind(): return lax.ppermute(block, axis, route)  37.4 us
    ppermute x8, waiting for transfers between devices, from_behind(): return lax.ppermute(block, axis, route)  37.1 us
    all_gather x1, waiting for transfers between devices, shards(): lax.all_gather(old_low, 'seq', axis=1, tiled=True)  25.6 us
    dot_general x12, matrix products, gram_times(): return jnp.einsum('mij,mjk->mik', row_block, gram_matrix, precision=precise)  23.2 us
    all_to_all x1, blocking collectives, shards(): lax.all_to_all(combined, 'head', split_axis=0, concat_axis=1, tiled=True)  7 us
    all_to_all x1, waiting for transfers between devices, shards(): lax.all_to_all(qkv, 'head', split_axis=2, concat_axis=1, tiled=True)  6.67 us
    dot_general x5, matrix products, contract_last(): lax.dot_general(left_side, right_side, (((1,), (1,)), ((), ())), preferre...  5.86 us
  transfers between devices with their start and end apart: 12, of which 9 were waited for; matrix products, arithmetic and copies ran while one was open for 2% of the time, Pallas kernels for 0%

commit v1 on v0

--- a/solution.py
+++ b/solution.py
@@ -83,7 +83,9 @@
     partial_value = head_gradient(
         key_norm, signal, lax.all_gather(old_low, "seq", axis=1, tiled=True)
     )
-    summed = lax.psum(partial_value, "seq")
+    summed = partial_value
+    for hop in (1, 2, 4, 8):
+        summed = summed + lax.ppermute(summed, "seq", [(dev, dev ^ hop) for dev in range(16)])
     frob_norm = jnp.sqrt(jnp.sum(summed * summed, axis=(1, 2), keepdims=True))
     normalized = summed / (frob_norm + norm_eps)
     gram_matrix = jnp.einsum("mij,mkj->mik", normalized, normalized, precision=precise)

time: 290 us -> 471 us (1.62)
  waiting for transfers between devices: 172 us -> 346 us
    ppermute x0 -> x4, waiting for transfers between devices: none -> 275 us  [shards(): lax.ppermute(summed, 'seq', [(dev, dev ^ hop) for dev in range(16)])]
    psum x1 -> x0, waiting for transfers between devices: 103 us -> none  [shards(): summed = lax.psum(partial_value, 'seq')]
    ppermute x0 -> x4, starting transfers between devices: none -> 5.3 us  [shards(): lax.ppermute(summed, 'seq', [(dev, dev ^ hop) for dev in range(16)])]
  transfers between devices with their start and end apart: 12 -> 15, of which waited for: 9 -> 12; matrix products, arithmetic and copies ran while one was open for 2% -> 2% of each run, Pallas kernels for 0% -> 0%
where the time goes in v1:
time: 471 us; the launch traced here: 470 us
  waiting for transfers between devices  346 us (73%)
  starting transfers between devices  45.8 us (10%)
  matrix products  42.1 us (9%)
  between operations  15.2 us (3%)
  other arithmetic  9.23 us (2%)
  blocking collectives  6.85 us (1%)
  local copies, waits for them, and re-layouts  5.27 us (1%)
    ppermute x4, waiting for transfers between devices, shards(): lax.ppermute(summed, 'seq', [(dev, dev ^ hop) for dev in range(16)])  275 us
    ppermute x8, waiting for transfers between devices, from_behind(): return lax.ppermute(block, axis, route)  39.8 us
    ppermute x8, starting transfers between devices, from_behind(): return lax.ppermute(block, axis, route)  36.9 us
    all_gather x1, waiting for transfers between devices, shards(): lax.all_gather(old_low, 'seq', axis=1, tiled=True)  24.3 us
    dot_general x12, matrix products, gram_times(): return jnp.einsum('mij,mjk->mik', row_block, gram_matrix, precision=precise)  23.1 us
  transfers between devices with their start and end apart: 15, of which 12 were waited for; matrix products, arithmetic and copies ran while one was open for 2% of the time, Pallas kernels for 0%

profile of v1, /device:TPU:16, one launch (start us, length us, event | category | flops | bytes accessed | tf_op | source)
XLA Modules:
  0.0 470.3 jit_solution(15007523551045421581)
XLA Ops:
  11.9 3.5 all-to-all-start
  15.5 6.7 %all-to-all-done = bf16[2,2,49152]{2,1,0:T(2,128)(2,1)S(1)} async-done(((bf16[2,2,49152]{2,1,0:T(2,128)(2,1)}), bf16[2,2,49152]{2,1,0:T(2,128)(2,1)S(1)}, u32[]{:S(2)}, u32[]{:S(2)}) %all-to-all-start) | async-done | bytes 393248 | tf_op jit(solution)/shard_map/all_to_all | solution.py:73
  25.3 24.3 %all-gather.3.cloned.1.call-done = bf16[3,512,512]{2,1,0:T(8,128)(2,1)} async-done(((bf16[3,32,512]{2,1,0:T(8,128)(2,1)}), bf16[3,512,512]{2,1,0:T(8,128)(2,1)}) %all-gather.3.cloned.1.call-update) | async-done | bytes 1572880 | tf_op jit(solution)/shard_map/all_gather | solution.py:84
  55.3 5.4 %collective-permute-done.8 = f32[3,512,512]{2,1,0:T(8,128)S(1)} collective-permute-done((f32[3,512,512]{2,1,0:T(8,128)S(1)}, f32[3,512,512]{2,1,0:T(8,128)S(1)}, u32[]{:S(2)}, u32[]{:S(2)}) %collective-permute-start.8) | collective-permute-done | bytes 3145760 | tf_op jit(solution)/shard_map/ppermute | solution.py:88
  62.3 69.5 %collective-permute-done.9 = f32[3,512,512]{2,1,0:T(8,128)S(1)} collective-permute-done((f32[3,512,512]{2,1,0:T(8,128)S(1)}, f32[3,512,512]{2,1,0:T(8,128)S(1)}, u32[]{:S(2)}, u32[]{:S(2)}) %collective-permute-start.9) | collective-permute-done | bytes 3145760 | tf_op jit(solution)/shard_map/ppermute | solution.py:88
  133.0 2.1 collective-permute-start.10
  135.1 67.6 %collective-permute-done.10 = f32[3,512,512]{2,1,0:T(8,128)S(1)} collective-permute-done((f32[3,512,512]{2,1,0:T(8,128)S(1)}, f32[3,512,512]{2,1,0:T(8,128)S(1)}, u32[]{:S(2)}, u32[]{:S(2)}) %collective-permute-start.10) | collective-permute-done | bytes 3145760 | tf_op jit(solution)/shard_map/ppermute | solution.py:88
  203.5 2.1 collective-permute-start.11
  206.4 132.5 %collective-permute-done.11 = f32[3,512,512]{2,1,0:T(8,128)} collective-permute-done((f32[3,512,512]{2,1,0:T(8,128)S(1)}, f32[3,512,512]{2,1,0:T(8,128)}, u32[]{:S(2)}, u32[]{:S(2)}) %collective-permute-start.11) | collective-permute-done | bytes 3145760 | tf_op jit(solution)/shard_map/ppermute | solution.py:88
  338.9 2.5 multiply_reduce_fusion
  341.5 5.7 %fusion.15 = f32[3,512,512]{2,1,0:T(8,128)S(1)} fusion(f32[3,512,512]{2,1,0:T(8,128)S(1)} %get-tuple-element.15, f32[3]{0:T(128)S(1)} %sqrt_add_fusion), kind=kOutput, calls=%fused_computation.33 | convolution fusion | flops 4832624640 | bytes 6291468 | tf_op jit(solution)/shard_map/mij,mkj->mik/dot_general | solution.py:91
  347.1 1.9 fusion.35
  349.0 2.1 fusion.49
  351.1 1.9 fusion.12
  354.9 1.9 fusion.11
  362.5 2.1 fusion.53
  364.6 1.9 fusion.9
  370.3 2.7 fusion.47
  374.4 4.6 collective-permute-start.1
  379.1 1.9 collective-permute-start.2
  381.0 1.9 collective-permute-start.3
  383.0 1.9 collective-permute-start.4
  385.8 1.9 collective-permute-start.5
  387.7 4.0 collective-permute-done.1
  391.7 10.7 %collective-permute-start.6 = (bf16[2,128,512]{2,1,0:T(8,128)(2,1)S(1)}, bf16[2,128,512]{2,1,0:T(8,128)(2,1)S(1)}, u32[]{:S(2)}, u32[]{:S(2)}) collective-permute-start(bf16[2,128,512]{2,1,0:T(8,128)(2,1)S(1)} %bitcast.119), channel_id=1, source_target_pairs={{0,4},{2,6},{4,8},{6,10},{8,12},{10,14},{12,16},{14,18},{16,20},{1... | collective-permute-start | bytes 786440 | tf_op jit(solution)/shard_map/ppermute | solution.py:19
  402.4 12.7 %collective-permute-start.7 = (bf16[2,128,512]{2,1,0:T(8,128)(2,1)S(1)}, bf16[2,128,512]{2,1,0:T(8,128)(2,1)S(1)}, u32[]{:S(2)}, u32[]{:S(2)}) collective-permute-start(bf16[2,128,512]{2,1,0:T(8,128)(2,1)S(1)} %bitcast.120), channel_id=1, source_target_pairs={{0,2},{2,4},{4,6},{6,8},{8,10},{10,12},{12,14},{14,16},{16,18},{18... | collective-permute-start | bytes 786440 | tf_op jit(solution)/shard_map/ppermute | solution.py:19
  415.2 9.7 %collective-permute-done.4 = bf16[2,128,512]{2,1,0:T(8,128)(2,1)S(1)} collective-permute-done((bf16[2,128,512]{2,1,0:T(8,128)(2,1)S(1)}, bf16[2,128,512]{2,1,0:T(8,128)(2,1)S(1)}, u32[]{:S(2)}, u32[]{:S(2)}) %collective-permute-start.4) | collective-permute-done | bytes 262176 | tf_op jit(solution)/shard_map/ppermute | solution.py:19
  424.9 2.7 collective-permute-done.5
  427.6 19.8 %collective-permute-done.6 = bf16[2,128,512]{2,1,0:T(8,128)(2,1)S(1)} collective-permute-done((bf16[2,128,512]{2,1,0:T(8,128)(2,1)S(1)}, bf16[2,128,512]{2,1,0:T(8,128)(2,1)S(1)}, u32[]{:S(2)}, u32[]{:S(2)}) %collective-permute-start.6) | collective-permute-done | bytes 262176 | tf_op jit(solution)/shard_map/ppermute | solution.py:19
  447.4 2.7 collective-permute-done.7
  452.2 2.4 fusion.14
  456.0 6.8 %all_to_all.34 = bf16[2,64,512]{2,1,0:T(8,128)(2,1)S(1)} all-to-all(bf16[2,64,512]{2,1,0:T(8,128)(2,1)S(1)} %bitcast.127), channel_id=1, replica_groups=mesh['seq'=16,'head'=2] {'head'}, dimensions={0} | all-to-all | bytes 262144 | tf_op jit(solution)/shard_map/all_to_all | solution.py:123
  (71 shorter events, 34.9 us)
Async XLA Ops:
  7.2 8.2 %copy-start.3 = (f32[128,1]{0,1:T(1,128)S(1)}, f32[128,1]{0,1:T(1,128)}, u32[]{:S(2)}) copy-start(f32[128,1]{0,1:T(1,128)} %param.5) | copy-start | bytes 1540
  7.2 42.5 %all-gather.3.cloned.1.call-start = ((), (), s32[]{:S(2)}) async-start(), calls=%async_computation.2 | async-start | bytes 1671168 | tf_op jit(solution)/shard_map/all_gather | solution.py:84
  11.9 10.3 %all-to-all-start = ((bf16[2,2,49152]{2,1,0:T(2,128)(2,1)}), bf16[2,2,49152]{2,1,0:T(2,128)(2,1)S(1)}, u32[]{:S(2)}, u32[]{:S(2)}) async-start(bf16[2,2,49152]{2,1,0:T(2,128)(2,1)} %reshape.124), calls=%async_computation | async-start | bytes 786432 | tf_op jit(solution)/shard_map/all_to_all | solution.py:73
  15.3 435.5 %all-gather.5.cloned.1.call-start = ((), (), s32[]{:S(2)}) async-start(), calls=%async_computation.3 | async-start | bytes 1671168 | tf_op jit(solution)/shard_map/all_gather | solution.py:102
  55.0 5.7 %collective-permute-start.8 = (f32[3,512,512]{2,1,0:T(8,128)S(1)}, f32[3,512,512]{2,1,0:T(8,128)S(1)}, u32[]{:S(2)}, u32[]{:S(2)}) collective-permute-start(f32[3,512,512]{2,1,0:T(8,128)S(1)} %pad_maximum_fusion), channel_id=1, source_target_pairs={{0,2},{2,0},{4,6},{6,4},{8,10},{10,8},{12,14},{14,12},{16,18},{18,... | collective-permute-start | bytes 9437192 | tf_op jit(solution)/shard_map/ppermute | solution.py:88
  61.5 70.3 %collective-permute-start.9 = (f32[3,512,512]{2,1,0:T(8,128)S(1)}, f32[3,512,512]{2,1,0:T(8,128)S(1)}, u32[]{:S(2)}, u32[]{:S(2)}) collective-permute-start(f32[3,512,512]{2,1,0:T(8,128)S(1)} %fusion.45), channel_id=1, source_target_pairs={{0,4},{2,6},{4,0},{6,2},{8,12},{10,14},{12,8},{14,10},{16,20},{18,... | collective-permute-start | bytes 9437192 | tf_op jit(solution)/shard_map/ppermute | solution.py:88
  133.0 69.7 %collective-permute-start.10 = (f32[3,512,512]{2,1,0:T(8,128)S(1)}, f32[3,512,512]{2,1,0:T(8,128)S(1)}, u32[]{:S(2)}, u32[]{:S(2)}) collective-permute-start(f32[3,512,512]{2,1,0:T(8,128)S(1)} %fusion.88), channel_id=1, source_target_pairs={{0,8},{2,10},{4,12},{6,14},{8,0},{10,2},{12,4},{14,6},{16,24},{18,... | collective-permute-start | bytes 9437192 | tf_op jit(solution)/shard_map/ppermute | solution.py:88
  203.5 135.5 %collective-permute-start.11 = (f32[3,512,512]{2,1,0:T(8,128)S(1)}, f32[3,512,512]{2,1,0:T(8,128)}, u32[]{:S(2)}, u32[]{:S(2)}) collective-permute-start(f32[3,512,512]{2,1,0:T(8,128)S(1)} %add.147), channel_id=1, source_target_pairs={{0,16},{2,18},{4,20},{6,22},{8,24},{10,26},{12,28},{14,30},{16,0},... | collective-permute-start | bytes 9437192 | tf_op jit(solution)/shard_map/ppermute | solution.py:88
  366.5 3.8 copy-start.1
  373.1 77.1 %copy-start.2 = (bf16[1,2,64,512]{3,2,1,0:T(8,128)(2,1)S(1)}, bf16[1,2,64,512]{3,2,1,0:T(8,128)(2,1)}, u32[]{:S(2)}) copy-start(bf16[1,2,64,512]{3,2,1,0:T(8,128)(2,1)} %get-tuple-element.16) | copy-start | bytes 393220
  373.1 12.7 %collective-permute-start = (bf16[2,128,512]{2,1,0:T(8,128)(2,1)S(1)}, bf16[2,128,512]{2,1,0:T(8,128)(2,1)S(1)}, u32[]{:S(2)}, u32[]{:S(2)}) collective-permute-start(bf16[2,128,512]{2,1,0:T(8,128)(2,1)S(1)} %bitcast.113), channel_id=1, source_target_pairs={{0,16},{2,18},{4,20},{6,22},{8,24},{10,26},{12,28},{14,30},{1,17},... | collective-permute-start | bytes 786440 | tf_op jit(solution)/shard_map/ppermute | solution.py:19
  374.4 17.3 %collective-permute-start.1 = (bf16[2,128,512]{2,1,0:T(8,128)(2,1)S(1)}, bf16[2,128,512]{2,1,0:T(8,128)(2,1)S(1)}, u32[]{:S(2)}, u32[]{:S(2)}) collective-permute-start(bf16[2,128,512]{2,1,0:T(8,128)(2,1)S(1)} %bitcast.114), channel_id=1, source_target_pairs={{0,14},{2,16},{4,18},{6,20},{8,22},{10,24},{12,26},{14,28},{16,30}... | collective-permute-start | bytes 786440 | tf_op jit(solution)/shard_map/ppermute | solution.py:19
  379.1 23.3 %collective-permute-start.2 = (bf16[2,128,512]{2,1,0:T(8,128)(2,1)S(1)}, bf16[2,128,512]{2,1,0:T(8,128)(2,1)S(1)}, u32[]{:S(2)}, u32[]{:S(2)}) collective-permute-start(bf16[2,128,512]{2,1,0:T(8,128)(2,1)S(1)} %bitcast.115), channel_id=1, source_target_pairs={{0,12},{2,14},{4,16},{6,18},{8,20},{10,22},{12,24},{14,26},{16,28}... | collective-permute-start | bytes 786440 | tf_op jit(solution)/shard_map/ppermute | solution.py:19
  381.0 34.1 %collective-permute-start.3 = (bf16[2,128,512]{2,1,0:T(8,128)(2,1)S(1)}, bf16[2,128,512]{2,1,0:T(8,128)(2,1)S(1)}, u32[]{:S(2)}, u32[]{:S(2)}) collective-permute-start(bf16[2,128,512]{2,1,0:T(8,128)(2,1)S(1)} %bitcast.116), channel_id=1, source_target_pairs={{0,10},{2,12},{4,14},{6,16},{8,18},{10,20},{12,22},{14,24},{16,26}... | collective-permute-start | bytes 786440 | tf_op jit(solution)/shard_map/ppermute | solution.py:19
  383.0 41.9 %collective-permute-start.4 = (bf16[2,128,512]{2,1,0:T(8,128)(2,1)S(1)}, bf16[2,128,512]{2,1,0:T(8,128)(2,1)S(1)}, u32[]{:S(2)}, u32[]{:S(2)}) collective-permute-start(bf16[2,128,512]{2,1,0:T(8,128)(2,1)S(1)} %bitcast.117), channel_id=1, source_target_pairs={{0,8},{2,10},{4,12},{6,14},{8,16},{10,18},{12,20},{14,22},{16,24},... | collective-permute-start | bytes 786440 | tf_op jit(solution)/shard_map/ppermute | solution.py:19
  385.8 41.8 %collective-permute-start.5 = (bf16[2,128,512]{2,1,0:T(8,128)(2,1)S(1)}, bf16[2,128,512]{2,1,0:T(8,128)(2,1)S(1)}, u32[]{:S(2)}, u32[]{:S(2)}) collective-permute-start(bf16[2,128,512]{2,1,0:T(8,128)(2,1)S(1)} %bitcast.118), channel_id=1, source_target_pairs={{0,6},{2,8},{4,10},{6,12},{8,14},{10,16},{12,18},{14,20},{16,22},{... | collective-permute-start | bytes 786440 | tf_op jit(solution)/shard_map/ppermute | solution.py:19
  391.7 55.7 %collective-permute-start.6 = (bf16[2,128,512]{2,1,0:T(8,128)(2,1)S(1)}, bf16[2,128,512]{2,1,0:T(8,128)(2,1)S(1)}, u32[]{:S(2)}, u32[]{:S(2)}) collective-permute-start(bf16[2,128,512]{2,1,0:T(8,128)(2,1)S(1)} %bitcast.119), channel_id=1, source_target_pairs={{0,4},{2,6},{4,8},{6,10},{8,12},{10,14},{12,16},{14,18},{16,20},{1... | collective-permute-start | bytes 786440 | tf_op jit(solution)/shard_map/ppermute | solution.py:19
  402.4 47.7 %collective-permute-start.7 = (bf16[2,128,512]{2,1,0:T(8,128)(2,1)S(1)}, bf16[2,128,512]{2,1,0:T(8,128)(2,1)S(1)}, u32[]{:S(2)}, u32[]{:S(2)}) collective-permute-start(bf16[2,128,512]{2,1,0:T(8,128)(2,1)S(1)} %bitcast.120), channel_id=1, source_target_pairs={{0,2},{2,4},{4,6},{6,8},{8,10},{10,12},{12,14},{14,16},{16,18},{18... | collective-permute-start | bytes 786440 | tf_op jit(solution)/shard_map/ppermute | solution.py:19
  415.2 35.7 %copy-start = (bf16[1,2,64,512]{3,2,1,0:T(8,128)(2,1)S(1)}, bf16[1,2,64,512]{3,2,1,0:T(8,128)(2,1)}, u32[]{:S(2)}) copy-start(bf16[1,2,64,512]{3,2,1,0:T(8,128)(2,1)} %get-tuple-element.20) | copy-start | bytes 393220
Sparse Core Ops, SparseCore 0:
  10.7 38.8 all-gather.2
  373.2 50.3 all-gather.4
